TPU v7x, 32 devices: a whole 2x2x4 slice. The times are simulated.
32 devices in a mesh: groups: 2 (over y), ep: 16 (over z, x, core).
Axes of the slice: x: 2, y: 2, z: 4, core: 2. Of those that a mesh axis runs over, the one named last changes fastest.
Arguments:
- queries: bfloat16 [64, 128, 576], P(('groups', 'ep')), parts along dimension 0, may hold values from -120 to 120
- kv_cache: bfloat16 [64, 256, 576], P(('groups', 'ep')), parts along dimension 0, may hold values from -6 to 6
- kv_lengths: int32 [64], P(('groups', 'ep')), parts along dimension 0, may hold values from 32 to 256, as said below
- moe_input: bfloat16 [64, 7168], P(('groups', 'ep')), parts along dimension 0, may hold values from -6 to 6
- expert_ids: int32 [64, 8], P(('groups', 'ep')), parts along dimension 0, may hold values from 0 to 15, all different within a row; in each aligned block of 2 rows (0 to 1, 2 to 3, ...) at most 2 rows name the same one
- route_weights: float32 [64, 8], P(('groups', 'ep')), parts along dimension 0, may hold values from 0.1 to 1
- w_gate: bfloat16 [32768, 7168], P('ep'), may hold values from -0.0625 to 0.0625
- w_up: bfloat16 [32768, 7168], P('ep'), may hold values from -0.0625 to 0.0625
- w_down: bfloat16 [32768, 7168], P('ep'), may hold values from -0.125 to 0.125
Outputs:
- attended: bfloat16 [64, 128, 512], P(('groups', 'ep')), parts along dimension 0
- moe_output: bfloat16 [64, 7168], P(('groups', 'ep')), parts along dimension 0
There are 2 independent parts, one for each index of `groups`. A program takes and returns all parts, laid end to end along the dimension named above; an argument that names none is the same for every part. Nothing has to cross between parts.
Inputs may be any that keep to these rules, and one draw needn't show every extreme that they name: `expert_ids`: the 8 ids of a row differ. Among the 2 rows of one device no expert is named more than 2 times, and in every draw some expert is named exactly 2 times by the rows of some device. `kv_lengths`: some request in every draw uses all 256 slots.
All inputs are finite; a program needn't handle non-finite values.
Results may differ from a plain program's by a relative error of at most 0.0085.
Values may be sent and summed in bfloat16 or wider, within the bound.
No kernel may reach another device: no remote copies, remote signals or barrier semaphores. Data moves between devices by JAX's collectives and lax.ppermute only.
A program may use at most 128 MiB of HBM per device.

v0:
```python
import jax
import jax.numpy as jnp
from jax import lax
from jax.sharding import PartitionSpec as P

LAT = 512
EXPERTS = 16
CAP = 2


score_scale = 192.0 ** (-0.5)


def attend_latent(queries, kv_cache, kv_lengths):
    scores = (
        jnp.einsum("rhk,rlk->rhl", queries, kv_cache, preferred_element_type=jnp.float32)
        * score_scale
    )
    slot_index = lax.broadcasted_iota(jnp.int32, scores.shape, 2)
    usable = slot_index < kv_lengths[:, None, None]
    scores = jnp.where(usable, scores, -1e30)
    row_max = jnp.max(scores, axis=2, keepdims=True)
    raw_weights = jnp.where(usable, jnp.exp(scores - row_max), 0.0)
    probs = (raw_weights / jnp.sum(raw_weights, axis=2, keepdims=True)).astype(jnp.bfloat16)
    values = kv_cache[:, :, :LAT]
    return jnp.einsum("rhl,rlk->rhk", probs, values, preferred_element_type=jnp.float32).astype(
        jnp.bfloat16
    )


def expert_rows(received, w_gate, w_up, w_down):
    flattened = received.reshape(-1, received.shape[-1])
    contract = (((1,), (1,)), ((), ()))
    gate_act = lax.dot_general(flattened, w_gate, contract, preferred_element_type=jnp.float32)
    up_act = lax.dot_general(flattened, w_up, contract, preferred_element_type=jnp.float32)
    hidden = (jax.nn.silu(gate_act) * up_act).astype(jnp.bfloat16)
    partial_out = jnp.dot(hidden, w_down, preferred_element_type=jnp.float32)
    return partial_out.reshape(received.shape[0], received.shape[1], partial_out.shape[-1])


def return_rows(partial_out):
    return lax.all_to_all(
        partial_out.astype(jnp.bfloat16), "ep", split_axis=0, concat_axis=0, tiled=True
    ).astype(partial_out.dtype)


def slot_map(member, capacity):
    position = jnp.cumsum(member, axis=-1) - member
    slot_ids = lax.broadcasted_iota(jnp.int32, (capacity, member.shape[-1]), 0)
    return member[..., None, :] * (position[..., None, :] == slot_ids).astype(jnp.int32)


def local(
    queries, kv_cache, kv_lengths, moe_input, expert_ids, route_weights, w_gate, w_up, w_down
):
    attended = attend_latent(queries, kv_cache, kv_lengths)
    devices = lax.axis_size("ep")
    slices = devices // EXPERTS
    requests = moe_input.shape[0]
    width = moe_input.shape[1]
    experts_iota = jnp.arange(EXPERTS, dtype=jnp.int32)
    matches = expert_ids[None, :, :] == experts_iota[:, None, None]
    member = jnp.sum(matches.astype(jnp.int32), axis=2)
    own_slots = slot_map(member, CAP)
    compact = jnp.einsum(
        "ecr,rd->ecd", own_slots.astype(jnp.bfloat16), moe_input, preferred_element_type=jnp.float32
    ).astype(jnp.bfloat16)
    outgoing = jnp.broadcast_to(compact[:, None], (EXPERTS, slices, CAP, width)).reshape(
        devices, CAP, width
    )
    returned = return_rows(
        expert_rows(
            lax.all_to_all(outgoing, "ep", split_axis=0, concat_axis=0, tiled=True),
            w_gate,
            w_up,
            w_down,
        )
    )
    summed = returned.reshape(EXPERTS, slices, CAP, width).sum(axis=1)
    weight_by_expert = jnp.sum(jnp.where(matches, route_weights[None, :, :], 0.0), axis=2)
    mixing = (own_slots.astype(jnp.float32) * weight_by_expert[:, None, :]).reshape(
        EXPERTS * CAP, requests
    )
    moe_output = lax.dot_general(
        mixing,
        summed.reshape(EXPERTS * CAP, width),
        (((0,), (0,)), ((), ())),
        precision=lax.Precision.HIGHEST,
        preferred_element_type=jnp.float32,
    )
    return (attended, moe_output.astype(jnp.bfloat16))


def solution(mesh):
    in_specs = (
        P(("groups", "ep"), None, None),
        P(("groups", "ep"), None, None),
        P(("groups", "ep")),
        P(("groups", "ep"), None),
        P(("groups", "ep"), None),
        P(("groups", "ep"), None),
        P("ep", None),
        P("ep", None),
        P("ep", None),
    )
    out_specs = (P(("groups", "ep"), None, None), P(("groups", "ep"), None))
    return jax.shard_map(local, mesh=mesh, in_specs=in_specs, out_specs=out_specs, check_vma=False)
```

profile of v0, /device:TPU:0, one launch (start us, length us, event | category | flops | bytes accessed | tf_op | source)
XLA Modules:
  0.0 78.9 jit_solution(7835878111630486628)
XLA Ops:
  0.6 0.0 copy-start
  0.6 0.8 %convert_reduce_fusion = s32[16,2]{0,1:T(2,128)S(1)} fusion(s32[2,8]{1,0:T(2,128)} %param.13), kind=kLoop, calls=%fused_computation.26 | loop fusion | flops 736 | bytes 192 | tf_op jit(solution)/shard_map/reduce_sum | solution.py:63
  1.5 1.1 %convolution_convert_fusion.1 = bf16[16,2,7168]{2,0,1:T(8,128)(2,1)S(1)} fusion(bf16[2,7168]{1,0:T(2,128)(2,1)} %param.12, s32[16,2]{0,1:T(2,128)S(1)} %convert_reduce_fusion, s32[16,2]{0,1:T(2,128)S(1)} %sub.17), kind=kOutput, calls=%fused_computation.2 | convolution fusion | flops 1147072 | bytes 487680 | tf_op jit(solution)/shard_map/ecr,rd->ecd/dot_general | solution.py:65
  2.6 0.5 copy.20
  3.1 20.4 %all_to_all.10 = bf16[16,2,7168]{2,1,0:T(2,128)(2,1)S(1)} all-to-all(bf16[16,2,7168]{2,1,0:T(2,128)(2,1)S(1)} %copy.20), channel_id=1, replica_groups=mesh['groups'=2,'ep'=16] {'ep'}, dimensions={0} | all-to-all | bytes 917504 | tf_op jit(solution)/shard_map/all_to_all | solution.py:73
  23.5 0.2 reshape.31
  23.6 14.0 %fusion.34 = f32[32,2048]{1,0:T(8,128)S(1)} fusion(bf16[32,7168]{1,0:T(8,128)(2,1)S(1)} %reshape.31, bf16[2048,7168]{1,0:T(8,128)(2,1)} %param.15), kind=kOutput, calls=%fused_computation.45 | convolution fusion | flops 939524096 | bytes 30081024 | tf_op jit(solution)/shard_map/dot_general | solution.py:34
  37.7 0.0 copy-start.2
  37.7 0.0 copy-start.3
  37.7 0.0 copy-start.1
  37.7 0.0 copy-start.4
  37.7 22.2 %convolution_convert_fusion = bf16[32,7168]{1,0:T(8,128)(2,1)S(1)} fusion(bf16[2048,7168]{1,0:T(8,128)(2,1)} %param.17, bf16[32,7168]{1,0:T(8,128)(2,1)S(1)} %reshape.31, bf16[2048,7168]{1,0:T(8,128)(2,1)} %param.16, f32[32,2048]{1,0:T(8,128)S(1)} %fusion.34), kind=kOutput, calls=%fused_computation.1 | convolution fusion | flops 1879670784 | bytes 59899904 | tf_op jit(solution)/shard_map/dot_general | solution.py:37
  59.9 0.9 %convert_element_type.40 = bf16[16,2,7168]{2,1,0:T(2,128)(2,1)} reshape(bf16[32,7168]{1,0:T(8,128)(2,1)S(1)} %convolution_convert_fusion) | data formatting | bytes 917504 | tf_op jit(solution)/shard_map/convert_element_type | solution.py:43
  60.9 3.8 %all-to-all-start.1 = ((bf16[16,2,7168]{2,1,0:T(2,128)(2,1)}), bf16[16,2,7168]{2,1,0:T(2,128)(2,1)S(1)}, u32[]{:S(2)}, u32[]{:S(2)}) async-start(bf16[16,2,7168]{2,1,0:T(2,128)(2,1)} %convert_element_type.40), calls=%async_computation.1 | async-start | bytes 917504 | tf_op jit(solution)/shard_map/all_to_all | solution.py:42
  64.7 0.0 copy-done.2
  64.7 0.0 copy-done.3
  64.7 0.1 select_reduce_fusion
  64.8 0.0 copy-done
  64.8 0.0 copy-done.1
  64.8 0.0 copy-done.4
  64.8 0.3 fusion.6
  65.1 0.2 fusion.33
  65.3 1.2 %convolution_convert_fusion.2 = bf16[2,128,512]{2,1,0:T(8,128)(2,1)} fusion(bf16[2,256,576]{1,2,0:T(8,128)(2,1)S(1)} %copy-done.1, f32[2,128]{1,0:T(2,128)S(1)} %fusion.33, f32[2,128,256]{2,1,0:T(8,128)S(1)} %fusion.6, s32[2]{0:T(128)S(1)} %copy-done.4), kind=kOutput, calls=%fused_computation.8 | convolution fusion | flops 67568128 | bytes 1312256 | tf_op jit(solution)/shard_map/rhl,rlk->rhk/dot_general | solution.py:26
  66.6 11.3 %all-to-all-done.1 = bf16[16,2,7168]{2,1,0:T(2,128)(2,1)S(1)} async-done(((bf16[16,2,7168]{2,1,0:T(2,128)(2,1)}), bf16[16,2,7168]{2,1,0:T(2,128)(2,1)S(1)}, u32[]{:S(2)}, u32[]{:S(2)}) %all-to-all-start.1) | async-done | bytes 458784 | tf_op jit(solution)/shard_map/all_to_all | solution.py:42
  77.9 1.0 %fusion.1 = bf16[2,7168]{1,0:T(2,128)(2,1)} fusion(bf16[16,2,7168]{2,1,0:T(2,128)(2,1)S(1)} %all-to-all-done.1, f32[16,2]{0,1:T(2,128)S(1)} %select_reduce_fusion, s32[16,2]{0,1:T(2,128)S(1)} %convert_reduce_fusion, s32[16,2]{0,1:T(2,128)S(1)} %sub.17), kind=kOutput, calls=%fused_computation.4 | convolution fusion | flops 5519616 | bytes 487808 | tf_op jit(solution)/shard_map/dot_general | solution.py:84
  (2 shorter events, 0.0 us)
Async XLA Ops:
  0.6 64.2 %copy-start = (bf16[2,128,576]{1,2,0:T(8,128)(2,1)S(1)}, bf16[2,128,576]{1,2,0:T(8,128)(2,1)}, u32[]{:S(2)}) copy-start(bf16[2,128,576]{1,2,0:T(8,128)(2,1)} %param.9) | copy-start | bytes 884740
  37.7 27.0 %copy-start.2 = (s32[2,8]{1,0:T(2,128)S(1)}, s32[2,8]{1,0:T(2,128)}, u32[]{:S(2)}) copy-start(s32[2,8]{1,0:T(2,128)} %param.13) | copy-start | bytes 196
  37.7 27.0 %copy-start.3 = (f32[2,8]{1,0:T(2,128)S(1)}, f32[2,8]{1,0:T(2,128)}, u32[]{:S(2)}) copy-start(f32[2,8]{1,0:T(2,128)} %param.14) | copy-start | bytes 196
  37.7 27.1 %copy-start.1 = (bf16[2,256,576]{1,2,0:T(8,128)(2,1)S(1)}, bf16[2,256,576]{1,2,0:T(8,128)(2,1)}, u32[]{:S(2)}) copy-start(bf16[2,256,576]{1,2,0:T(8,128)(2,1)} %param.10) | copy-start | bytes 1769476
  37.7 27.1 %copy-start.4 = (s32[2]{0:T(128)S(1)}, s32[2]{0:T(128)}, u32[]{:S(2)}) copy-start(s32[2]{0:T(128)} %param.11) | copy-start | bytes 28
  60.9 17.0 %all-to-all-start.1 = ((bf16[16,2,7168]{2,1,0:T(2,128)(2,1)}), bf16[16,2,7168]{2,1,0:T(2,128)(2,1)S(1)}, u32[]{:S(2)}, u32[]{:S(2)}) async-start(bf16[16,2,7168]{2,1,0:T(2,128)(2,1)} %convert_element_type.40), calls=%async_computation.1 | async-start | bytes 917504 | tf_op jit(solution)/shard_map/all_to_all | solution.py:42
where the time goes:
time: 79.2 us; the launch traced here: 78.9 us
  matrix products  39.8 us (50%)
  blocking collectives  20.4 us (26%)
  waiting for transfers between devices  11.3 us (14%)
  starting transfers between devices  3.8 us (5%)
  local copies, waits for them, and re-layouts  1.63 us (2%)
  other arithmetic  1.16 us (1%)
    dot_general x1, matrix products, expert_rows(): partial_out = jnp.dot(hidden, w_down, preferred_element_type=jnp.float32)  22.2 us
    all_to_all x1, blocking collectives, local(): lax.all_to_all(outgoing, 'ep', split_axis=0, concat_axis=0, tiled=True)  20.4 us
    dot_general x1, matrix products, expert_rows(): lax.dot_general(flattened, w_gate, contract, preferred_element_type=jnp.f...  14 us
    all_to_all x1, waiting for transfers between devices, return_rows(): lax.all_to_all(partial_out.astype(jnp.bfloat16), 'ep', split_axis=0, conc...  11.3 us
    all_to_all x1, starting transfers between devices, return_rows(): lax.all_to_all(partial_out.astype(jnp.bfloat16), 'ep', split_axis=0, conc...  3.8 us
  transfers between devices with their start and end apart: 1, of which 1 were waited for; matrix products, arithmetic and copies ran while one was open for 2% of the time, Pallas kernels for 0%

commit v1 on v0

v1 whole, which is shorter than its diff:
```python
import functools

import jax
import jax.numpy as jnp
from jax import lax
from jax.experimental import pallas as pl
from jax.experimental.pallas import tpu as pltpu
from jax.sharding import PartitionSpec as P

LAT = 512
EXPERTS = 16
LANES = 128
HIDDEN_TILE = 256
COLUMN_TILE = 1024
SLOTS = 4

score_scale = 192.0 ** (-0.5)
rows_by_rows = (((1,), (1,)), ((), ()))


def attend_latent(queries, kv_cache, kv_lengths):
    scores = (
        jnp.einsum("rhk,rlk->rhl", queries, kv_cache, preferred_element_type=jnp.float32)
        * score_scale
    )
    slot_index = lax.broadcasted_iota(jnp.int32, scores.shape, 2)
    usable = slot_index < kv_lengths[:, None, None]
    scores = jnp.where(usable, scores, -1e30)
    row_max = jnp.max(scores, axis=2, keepdims=True)
    raw_weights = jnp.where(usable, jnp.exp(scores - row_max), 0.0)
    probs = (raw_weights / jnp.sum(raw_weights, axis=2, keepdims=True)).astype(jnp.bfloat16)
    values = kv_cache[:, :, :LAT]
    return jnp.einsum("rhl,rlk->rhk", probs, values, preferred_element_type=jnp.float32).astype(
        jnp.bfloat16
    )


def largest_tile(size, unit, most):
    return max(t for t in range(unit, min(size, most) + 1, unit) if size % t == 0)


def expert_kernel(width, hidden, expert_ref, own_ref, other_ref, *refs):
    w_gate, w_up, w_down, keep_ref, send_ref = refs[:5]
    tokens, gate_act, hid, row_buf, col_buf, row_sem, col_sem = refs[5:]
    half = own_ref.shape[0]
    tile, columns = row_buf.shape[1], col_buf.shape[2]
    row_slots, col_slots = row_buf.shape[0], col_buf.shape[0]
    row_tiles = 2 * (hidden // tile)
    col_tiles = width // columns

    def fetch(item):
        if item < row_tiles:
            source = (w_gate, w_up)[item % 2].at[pl.ds((item // 2) * tile, tile), :]
            slot = item % row_slots
            return pltpu.make_async_copy(source, row_buf.at[slot], row_sem.at[slot])
        item -= row_tiles
        slot = item % col_slots
        source = w_down.at[:, pl.ds(item * columns, columns)]
        return pltpu.make_async_copy(source, col_buf.at[slot], col_sem.at[slot])

    ahead = min(row_slots, col_slots)
    items = row_tiles + col_tiles
    for item in range(min(ahead, items)):
        fetch(item).start()
    tokens[pl.ds(0, half), :] = own_ref[...]
    tokens[pl.ds(half, half), :] = other_ref[...]

    for item in range(row_tiles):
        fetch(item).wait()
        act = lax.dot_general(
            tokens[:, pl.ds(0, width)],
            row_buf[item % row_slots],
            rows_by_rows,
            preferred_element_type=jnp.float32,
        )
        if item + ahead < items:
            fetch(item + ahead).start()
        if item % 2 == 0:
            gate_act[...] = act
        else:
            gated = gate_act[...]
            hid[:, pl.ds((item // 2) * tile, tile)] = (
                gated / (1.0 + jnp.exp(-gated)) * act
            ).astype(hid.dtype)

    extra = tokens[:, pl.ds(width, LANES)].astype(jnp.float32)
    lane = lax.broadcasted_iota(jnp.int32, extra.shape, 1)
    expert = expert_ref[0]
    mine = (lane == expert) | (lane == expert + EXPERTS)
    scale = jnp.sum(jnp.where(mine, extra, 0.0), axis=1, keepdims=True)

    for tile_id in range(col_tiles):
        item = row_tiles + tile_id
        fetch(item).wait()
        partial = jnp.dot(
            hid[...], col_buf[tile_id % col_slots], preferred_element_type=jnp.float32
        )
        if item + ahead < items:
            fetch(item + ahead).start()
        partial = partial * scale
        where = pl.ds(tile_id * columns, columns)
        keep_ref[:, where] = partial[:half]
        send_ref[:, where] = partial[half:].astype(send_ref.dtype)


def run_expert(expert, own, other, w_gate, w_up, w_down):
    half = own.shape[0]
    hidden, width = w_down.shape
    tile = largest_tile(hidden, LANES, HIDDEN_TILE)
    columns = largest_tile(width, LANES, COLUMN_TILE)
    in_vmem = pl.BlockSpec(memory_space=pltpu.VMEM)
    in_place = pl.BlockSpec(memory_space=pl.ANY)
    return pl.pallas_call(
        functools.partial(expert_kernel, width, hidden),
        out_shape=(
            jax.ShapeDtypeStruct((half, width), jnp.float32),
            jax.ShapeDtypeStruct((half, width), own.dtype),
        ),
        in_specs=[pl.BlockSpec(memory_space=pltpu.SMEM), in_vmem, in_vmem] + [in_place] * 3,
        out_specs=(in_vmem, in_vmem),
        scratch_shapes=[
            pltpu.VMEM((2 * half, own.shape[1]), own.dtype),
            pltpu.VMEM((2 * half, tile), jnp.float32),
            pltpu.VMEM((2 * half, hidden), own.dtype),
            pltpu.VMEM((SLOTS, tile, width), w_gate.dtype),
            pltpu.VMEM((SLOTS, hidden, columns), w_down.dtype),
            pltpu.SemaphoreType.DMA((SLOTS,)),
            pltpu.SemaphoreType.DMA((SLOTS,)),
        ],
        compiler_params=pltpu.CompilerParams(vmem_limit_bytes=44 << 20),
        cost_estimate=pl.CostEstimate(
            flops=12 * half * hidden * width,
            bytes_accessed=6 * hidden * width,
            transcendentals=2 * half * hidden,
        ),
        name="expert",
    )(expert, own, other, w_gate, w_up, w_down)


def swap(value, mask, devices):
    return lax.ppermute(value, "ep", [(i, i ^ mask) for i in range(devices)])


def local(
    queries, kv_cache, kv_lengths, moe_input, expert_ids, route_weights, w_gate, w_up, w_down
):
    attended = attend_latent(queries, kv_cache, kv_lengths)
    devices = lax.axis_size("ep")
    slices = devices // EXPERTS
    requests = moe_input.shape[0]

    experts_iota = jnp.arange(EXPERTS, dtype=jnp.int32)
    matches = expert_ids[:, :, None] == experts_iota[None, None, :]
    dense = jnp.sum(jnp.where(matches, route_weights[:, :, None], 0.0), axis=1)
    high = lax.reduce_precision(dense, 8, 7)
    parts = jnp.concatenate(
        [high, dense - high, jnp.zeros((requests, LANES - 2 * EXPERTS), jnp.float32)], axis=1
    )
    rows = jnp.concatenate([moe_input, parts.astype(moe_input.dtype)], axis=1)

    masks = [1 << bit for bit in range(devices.bit_length() - 1)]
    for mask in reversed(masks[1:]):
        rows = jnp.concatenate([rows, swap(rows, mask, devices)], axis=0)
    other = swap(rows, masks[0], devices)

    expert = (lax.axis_index("ep") // slices).astype(jnp.int32).reshape(1)
    keep, send = run_expert(expert, rows, other, w_gate, w_up, w_down)
    total = keep + swap(send, masks[0], devices).astype(jnp.float32)
    for mask in masks[1:]:
        half = total.shape[0] // 2
        arrived = swap(total[half:].astype(moe_input.dtype), mask, devices)
        total = total[:half] + arrived.astype(jnp.float32)
    return (attended, total.astype(jnp.bfloat16))


def solution(mesh):
    in_specs = (
        P(("groups", "ep"), None, None),
        P(("groups", "ep"), None, None),
        P(("groups", "ep")),
        P(("groups", "ep"), None),
        P(("groups", "ep"), None),
        P(("groups", "ep"), None),
        P("ep", None),
        P("ep", None),
        P("ep", None),
    )
    out_specs = (P(("groups", "ep"), None, None), P(("groups", "ep"), None))
    return jax.shard_map(local, mesh=mesh, in_specs=in_specs, out_specs=out_specs, check_vma=False)
```

time: 79.2 us -> 77.7 us (0.981)
  Pallas kernels: 0 us -> 41.1 us
  matrix products: 39.8 us -> 1.56 us
  blocking collectives: 20.4 us -> 0 us
  starting transfers between devices: 3.8 us -> 13.9 us
  waiting for transfers between devices: 11.3 us -> 17.1 us
  other arithmetic: 1.16 us -> 2.13 us
    pallas_call x0 -> x1, Pallas kernels: none -> 41.1 us  [run_expert(): pl.pallas_call(functools.partial(expert_kernel, width, hidden), out_shape...]
    dot_general x4 -> x0, matrix products: 38.3 us -> none  [the longest x1 22.2 us: expert_rows(): partial_out = jnp.dot(hidden, w_down, preferred_element_type=jnp.float32)]
    all_to_all x1 -> x0, blocking collectives: 20.4 us -> none  [local(): lax.all_to_all(outgoing, 'ep', split_axis=0, concat_axis=0, tiled=True)]
    ppermute x0 -> x8, waiting for transfers between devices: none -> 17.1 us  [swap(): return lax.ppermute(value, 'ep', [(i, i ^ mask) for i in range(devices)])]
    ppermute x0 -> x8, starting transfers between devices: none -> 13.9 us  [swap(): return lax.ppermute(value, 'ep', [(i, i ^ mask) for i in range(devices)])]
    all_to_all x1 -> x0, waiting for transfers between devices: 11.3 us -> none  [return_rows(): lax.all_to_all(partial_out.astype(jnp.bfloat16), 'ep', split_axis=0, conc...]
    all_to_all x1 -> x0, starting transfers between devices: 3.8 us -> none  [return_rows(): lax.all_to_all(partial_out.astype(jnp.bfloat16), 'ep', split_axis=0, conc...]
    convert_element_type x2 -> x0, local copies, waits for them, and re-layouts: 1.42 us -> none  [the longest x1 0.94 us: return_rows(): partial_out.astype(jnp.bfloat16)]
  transfers between devices with their start and end apart: 1 -> 8, of which waited for: 1 -> 8; matrix products, arithmetic and copies ran while one was open for 2% -> 2% of each run, Pallas kernels for 0% -> 0%
where the time goes in v1:
time: 77.7 us; the launch traced here: 77.5 us
  Pallas kernels  41.1 us (53%)
  waiting for transfers between devices  17.1 us (22%)
  starting transfers between devices  13.9 us (18%)
  other arithmetic  2.13 us (3%)
  matrix products  1.56 us (2%)
  local copies, waits for them, and re-layouts  0.94 us (1%)
    pallas_call x1, Pallas kernels, run_expert(): pl.pallas_call(functools.partial(expert_kernel, width, hidden), out_shape...  41.1 us
    ppermute x8, waiting for transfers between devices, swap(): return lax.ppermute(value, 'ep', [(i, i ^ mask) for i in range(devices)])  17.1 us
    ppermute x8, starting transfers between devices, swap(): return lax.ppermute(value, 'ep', [(i, i ^ mask) for i in range(devices)])  13.9 us
  transfers between devices with their start and end apart: 8, of which 8 were waited for; matrix products, arithmetic and copies ran while one was open for 2% of the time, Pallas kernels for 0%

profile of v1, /device:TPU:0, one launch (start us, length us, event | category | flops | bytes accessed | tf_op | source)
XLA Modules:
  0.0 77.5 jit_solution(16810998326089035118)
XLA Ops:
  0.6 0.0 copy-start
  0.6 0.8 %select_reduce_fusion = f32[2,16]{1,0:T(2,128)S(1)} fusion(f32[2,8]{1,0:T(2,128)} %param.14, s32[2,8]{1,0:T(2,128)} %param.13), kind=kLoop, calls=%fused_computation.22 | loop fusion | flops 736 | bytes 256 | tf_op jit(solution)/shard_map/reduce_sum | solution.py:154
  1.5 0.8 %concatenate.17 = bf16[2,7296]{1,0:T(2,128)(2,1)S(1)} concatenate(bf16[2,7168]{1,0:T(2,128)(2,1)} %param.12, bf16[2,16]{1,0:T(2,128)(2,1)S(1)} %get-tuple-element.7, bf16[2,16]{1,0:T(2,128)(2,1)S(1)} %get-tuple-element.6, bf16[2,96]{1,0:T(2,128)(2,1)S(1)} %broadcast_in_dim.32), dimensions={1} | concatenate | bytes 58368 | tf_op jit(solution)/shard_map/concatenate | solution.py:159
  2.3 4.1 %collective-permute-start = (bf16[2,7296]{1,0:T(2,128)(2,1)S(1)}, bf16[2,7296]{1,0:T(2,128)(2,1)S(1)}, u32[]{:S(2)}, u32[]{:S(2)}) collective-permute-start(bf16[2,7296]{1,0:T(2,128)(2,1)S(1)} %concatenate.17), channel_id=1, source_target_pairs={{0,8},{1,9},{2,10},{3,11},{4,12},{5,13},{6,14},{7,15},{8,0},{9,1},... | collective-permute-start | bytes 87560 | tf_op jit(solution)/shard_map/ppermute | solution.py:141
  6.4 2.2 %collective-permute-done = bf16[2,7296]{1,0:T(2,128)(2,1)S(1)} collective-permute-done((bf16[2,7296]{1,0:T(2,128)(2,1)S(1)}, bf16[2,7296]{1,0:T(2,128)(2,1)S(1)}, u32[]{:S(2)}, u32[]{:S(2)}) %collective-permute-start) | collective-permute-done | bytes 29216 | tf_op jit(solution)/shard_map/ppermute | solution.py:141
  8.6 0.1 pad_maximum_fusion.2
  8.7 1.7 %collective-permute-start.1 = (bf16[4,7296]{1,0:T(4,128)(2,1)S(1)}, bf16[4,7296]{1,0:T(4,128)(2,1)S(1)}, u32[]{:S(2)}, u32[]{:S(2)}) collective-permute-start(bf16[4,7296]{1,0:T(4,128)(2,1)S(1)} %pad_maximum_fusion.2), channel_id=1, source_target_pairs={{0,4},{1,5},{2,6},{3,7},{4,0},{5,1},{6,2},{7,3},{8,12},{9,13},{10,... | collective-permute-start | bytes 175112 | tf_op jit(solution)/shard_map/ppermute | solution.py:141
  10.3 2.6 %collective-permute-done.1 = bf16[4,7296]{1,0:T(4,128)(2,1)S(1)} collective-permute-done((bf16[4,7296]{1,0:T(4,128)(2,1)S(1)}, bf16[4,7296]{1,0:T(4,128)(2,1)S(1)}, u32[]{:S(2)}, u32[]{:S(2)}) %collective-permute-start.1) | collective-permute-done | bytes 58400 | tf_op jit(solution)/shard_map/ppermute | solution.py:141
  12.9 0.1 pad_maximum_fusion.1
  13.0 1.8 %collective-permute-start.2 = (bf16[8,7296]{1,0:T(8,128)(2,1)S(1)}, bf16[8,7296]{1,0:T(8,128)(2,1)S(1)}, u32[]{:S(2)}, u32[]{:S(2)}) collective-permute-start(bf16[8,7296]{1,0:T(8,128)(2,1)S(1)} %pad_maximum_fusion.1), channel_id=1, source_target_pairs={{0,2},{1,3},{2,0},{3,1},{4,6},{5,7},{6,4},{7,5},{8,10},{9,11},{10,... | collective-permute-start | bytes 350216 | tf_op jit(solution)/shard_map/ppermute | solution.py:141
  14.8 3.1 %collective-permute-done.2 = bf16[8,7296]{1,0:T(8,128)(2,1)S(1)} collective-permute-done((bf16[8,7296]{1,0:T(8,128)(2,1)S(1)}, bf16[8,7296]{1,0:T(8,128)(2,1)S(1)}, u32[]{:S(2)}, u32[]{:S(2)}) %collective-permute-start.2) | collective-permute-done | bytes 116768 | tf_op jit(solution)/shard_map/ppermute | solution.py:141
  17.9 0.2 pad_maximum_fusion.own_ref
  18.1 0.1 collective-permute-start.3
  18.2 1.5 %collective-permute-done.3.other_ref = bf16[16,7296]{1,0:T(8,128)(2,1)S(1)} collective-permute-done((bf16[16,7296]{1,0:T(8,128)(2,1)S(1)}, bf16[16,7296]{1,0:T(8,128)(2,1)S(1)}, u32[]{:S(2)}, u32[]{:S(2)}) %collective-permute-start.3) | collective-permute-done | bytes 233504 | tf_op jit(solution)/shard_map/ppermute | solution.py:141
  19.6 0.0 copy-start.1
  19.6 41.1 %expert.1 = (f32[16,7168]{1,0:T(8,128)S(1)}, bf16[16,7168]{1,0:T(8,128)(2,1)S(1)}) custom-call(s32[1]{0:T(128)} %bitcast.expert_ref, bf16[16,7296]{1,0:T(8,128)(2,1)S(1)} %pad_maximum_fusion.own_ref, bf16[16,7296]{1,0:T(8,128)(2,1)S(1)} %collective-permute-done.3.other_ref, bf16[2048,7168]{1,0:T(8,128)(2,1)} %refs_0_.1, bf16[2048,7168]{1,0:T(8,128)(2,1)} %refs_1_.1, ...), custom_call_target="tpu_custom_call" | custom-call | flops 2818572288 | bytes 88080384 | tf_op jit(solution)/shard_map/expert/pallas_call | solution.py:113
  60.7 0.2 collective-permute-start.4
  60.9 1.4 %collective-permute-done.4 = bf16[16,7168]{1,0:T(8,128)(2,1)S(1)} collective-permute-done((bf16[16,7168]{1,0:T(8,128)(2,1)S(1)}, bf16[16,7168]{1,0:T(8,128)(2,1)S(1)}, u32[]{:S(2)}, u32[]{:S(2)}) %collective-permute-start.4) | collective-permute-done | bytes 229408 | tf_op jit(solution)/shard_map/ppermute | solution.py:141
  62.3 0.1 convert_add_fusion
  62.4 1.8 %collective-permute-start.5 = (bf16[8,7168]{1,0:T(8,128)(2,1)S(1)}, bf16[8,7168]{1,0:T(8,128)(2,1)S(1)}, u32[]{:S(2)}, u32[]{:S(2)}) collective-permute-start(bf16[8,7168]{1,0:T(8,128)(2,1)S(1)} %slice.47), channel_id=1, source_target_pairs={{0,2},{1,3},{2,0},{3,1},{4,6},{5,7},{6,4},{7,5},{8,10},{9,11},{10,... | collective-permute-start | bytes 344072 | tf_op jit(solution)/shard_map/ppermute | solution.py:141
  64.1 0.0 copy-done
  64.1 0.0 copy-done.1
  64.1 0.0 copy-done.2
  64.1 0.3 fusion.4
  64.5 3.2 %collective-permute-done.5 = bf16[8,7168]{1,0:T(8,128)(2,1)S(1)} collective-permute-done((bf16[8,7168]{1,0:T(8,128)(2,1)S(1)}, bf16[8,7168]{1,0:T(8,128)(2,1)S(1)}, u32[]{:S(2)}, u32[]{:S(2)}) %collective-permute-start.5) | collective-permute-done | bytes 114720 | tf_op jit(solution)/shard_map/ppermute | solution.py:141
  67.7 1.7 %collective-permute-start.6 = (bf16[4,7168]{1,0:T(4,128)(2,1)S(1)}, bf16[4,7168]{1,0:T(4,128)(2,1)S(1)}, u32[]{:S(2)}, u32[]{:S(2)}) collective-permute-start(bf16[4,7168]{1,0:T(4,128)(2,1)S(1)} %slice.48), channel_id=1, source_target_pairs={{0,4},{1,5},{2,6},{3,7},{4,0},{5,1},{6,2},{7,3},{8,12},{9,13},{10,... | collective-permute-start | bytes 172040 | tf_op jit(solution)/shard_map/ppermute | solution.py:141
  69.3 0.2 fusion.11
  69.6 2.4 %collective-permute-done.6 = bf16[4,7168]{1,0:T(4,128)(2,1)S(1)} collective-permute-done((bf16[4,7168]{1,0:T(4,128)(2,1)S(1)}, bf16[4,7168]{1,0:T(4,128)(2,1)S(1)}, u32[]{:S(2)}, u32[]{:S(2)}) %collective-permute-start.6) | collective-permute-done | bytes 57376 | tf_op jit(solution)/shard_map/ppermute | solution.py:141
  72.0 2.7 %collective-permute-start.7 = (bf16[2,7168]{1,0:T(2,128)(2,1)S(1)}, bf16[2,7168]{1,0:T(2,128)(2,1)S(1)}, u32[]{:S(2)}, u32[]{:S(2)}) collective-permute-start(bf16[2,7168]{1,0:T(2,128)(2,1)S(1)} %slice.49), channel_id=1, source_target_pairs={{0,8},{1,9},{2,10},{3,11},{4,12},{5,13},{6,14},{7,15},{8,0},{9,1},... | collective-permute-start | bytes 86024 | tf_op jit(solution)/shard_map/ppermute | solution.py:141
  74.7 1.2 %convolution_convert_fusion = bf16[2,128,512]{2,1,0:T(8,128)(2,1)} fusion(bf16[2,256,576]{1,2,0:T(8,128)(2,1)S(1)} %copy-done.1, f32[2,128]{1,0:T(2,128)S(1)} %fusion.11, f32[2,128,256]{2,1,0:T(8,128)S(1)} %fusion.4, s32[2]{0:T(128)S(1)} %copy-done.2), kind=kOutput, calls=%fused_computation.2 | convolution fusion | flops 67568128 | bytes 1312256 | tf_op jit(solution)/shard_map/rhl,rlk->rhk/dot_general | solution.py:33
  75.9 0.9 %collective-permute-done.7 = bf16[2,7168]{1,0:T(2,128)(2,1)S(1)} collective-permute-done((bf16[2,7168]{1,0:T(2,128)(2,1)S(1)}, bf16[2,7168]{1,0:T(2,128)(2,1)S(1)}, u32[]{:S(2)}, u32[]{:S(2)}) %collective-permute-start.7) | collective-permute-done | bytes 28704 | tf_op jit(solution)/shard_map/ppermute | solution.py:141
  76.8 0.6 fusion.7
  (8 shorter events, 0.1 us)
Async XLA Ops:
  0.6 63.5 %copy-start = (bf16[2,128,576]{1,2,0:T(8,128)(2,1)S(1)}, bf16[2,128,576]{1,2,0:T(8,128)(2,1)}, u32[]{:S(2)}) copy-start(bf16[2,128,576]{1,2,0:T(8,128)(2,1)} %param.9) | copy-start | bytes 884740
  2.3 6.3 %collective-permute-start = (bf16[2,7296]{1,0:T(2,128)(2,1)S(1)}, bf16[2,7296]{1,0:T(2,128)(2,1)S(1)}, u32[]{:S(2)}, u32[]{:S(2)}) collective-permute-start(bf16[2,7296]{1,0:T(2,128)(2,1)S(1)} %concatenate.17), channel_id=1, source_target_pairs={{0,8},{1,9},{2,10},{3,11},{4,12},{5,13},{6,14},{7,15},{8,0},{9,1},... | collective-permute-start | bytes 87560 | tf_op jit(solution)/shard_map/ppermute | solution.py:141
  8.7 4.3 %collective-permute-start.1 = (bf16[4,7296]{1,0:T(4,128)(2,1)S(1)}, bf16[4,7296]{1,0:T(4,128)(2,1)S(1)}, u32[]{:S(2)}, u32[]{:S(2)}) collective-permute-start(bf16[4,7296]{1,0:T(4,128)(2,1)S(1)} %pad_maximum_fusion.2), channel_id=1, source_target_pairs={{0,4},{1,5},{2,6},{3,7},{4,0},{5,1},{6,2},{7,3},{8,12},{9,13},{10,... | collective-permute-start | bytes 175112 | tf_op jit(solution)/shard_map/ppermute | solution.py:141
  13.0 4.9 %collective-permute-start.2 = (bf16[8,7296]{1,0:T(8,128)(2,1)S(1)}, bf16[8,7296]{1,0:T(8,128)(2,1)S(1)}, u32[]{:S(2)}, u32[]{:S(2)}) collective-permute-start(bf16[8,7296]{1,0:T(8,128)(2,1)S(1)} %pad_maximum_fusion.1), channel_id=1, source_target_pairs={{0,2},{1,3},{2,0},{3,1},{4,6},{5,7},{6,4},{7,5},{8,10},{9,11},{10,... | collective-permute-start | bytes 350216 | tf_op jit(solution)/shard_map/ppermute | solution.py:141
  18.1 1.6 %collective-permute-start.3 = (bf16[16,7296]{1,0:T(8,128)(2,1)S(1)}, bf16[16,7296]{1,0:T(8,128)(2,1)S(1)}, u32[]{:S(2)}, u32[]{:S(2)}) collective-permute-start(bf16[16,7296]{1,0:T(8,128)(2,1)S(1)} %pad_maximum_fusion.own_ref), channel_id=1, source_target_pairs={{0,1},{1,0},{2,3},{3,2},{4,5},{5,4},{6,7},{7,6},{8,9},{9,8},{10,11... | collective-permute-start | bytes 700424 | tf_op jit(solution)/shard_map/ppermute | solution.py:141
  19.6 44.5 %copy-start.1 = (bf16[2,256,576]{1,2,0:T(8,128)(2,1)S(1)}, bf16[2,256,576]{1,2,0:T(8,128)(2,1)}, u32[]{:S(2)}) copy-start(bf16[2,256,576]{1,2,0:T(8,128)(2,1)} %param.10) | copy-start | bytes 1769476
  19.6 44.5 %copy-start.2 = (s32[2]{0:T(128)S(1)}, s32[2]{0:T(128)}, u32[]{:S(2)}) copy-start(s32[2]{0:T(128)} %param.11) | copy-start | bytes 28
  60.7 1.6 %collective-permute-start.4 = (bf16[16,7168]{1,0:T(8,128)(2,1)S(1)}, bf16[16,7168]{1,0:T(8,128)(2,1)S(1)}, u32[]{:S(2)}, u32[]{:S(2)}) collective-permute-start(bf16[16,7168]{1,0:T(8,128)(2,1)S(1)} %get-tuple-element.5), channel_id=1, source_target_pairs={{0,1},{1,0},{2,3},{3,2},{4,5},{5,4},{6,7},{7,6},{8,9},{9,8},{10,11... | collective-permute-start | bytes 688136 | tf_op jit(solution)/shard_map/ppermute | solution.py:141
  62.4 5.3 %collective-permute-start.5 = (bf16[8,7168]{1,0:T(8,128)(2,1)S(1)}, bf16[8,7168]{1,0:T(8,128)(2,1)S(1)}, u32[]{:S(2)}, u32[]{:S(2)}) collective-permute-start(bf16[8,7168]{1,0:T(8,128)(2,1)S(1)} %slice.47), channel_id=1, source_target_pairs={{0,2},{1,3},{2,0},{3,1},{4,6},{5,7},{6,4},{7,5},{8,10},{9,11},{10,... | collective-permute-start | bytes 344072 | tf_op jit(solution)/shard_map/ppermute | solution.py:141
  67.7 4.2 %collective-permute-start.6 = (bf16[4,7168]{1,0:T(4,128)(2,1)S(1)}, bf16[4,7168]{1,0:T(4,128)(2,1)S(1)}, u32[]{:S(2)}, u32[]{:S(2)}) collective-permute-start(bf16[4,7168]{1,0:T(4,128)(2,1)S(1)} %slice.48), channel_id=1, source_target_pairs={{0,4},{1,5},{2,6},{3,7},{4,0},{5,1},{6,2},{7,3},{8,12},{9,13},{10,... | collective-permute-start | bytes 172040 | tf_op jit(solution)/shard_map/ppermute | solution.py:141
  72.0 4.8 %collective-permute-start.7 = (bf16[2,7168]{1,0:T(2,128)(2,1)S(1)}, bf16[2,7168]{1,0:T(2,128)(2,1)S(1)}, u32[]{:S(2)}, u32[]{:S(2)}) collective-permute-start(bf16[2,7168]{1,0:T(2,128)(2,1)S(1)} %slice.49), channel_id=1, source_target_pairs={{0,8},{1,9},{2,10},{3,11},{4,12},{5,13},{6,14},{7,15},{8,0},{9,1},... | collective-permute-start | bytes 86024 | tf_op jit(solution)/shard_map/ppermute | solution.py:141
